TPU v7x, 128 devices: a whole 4x4x4 slice. The times are simulated.
128 devices in a mesh: frame: 8 (over z_lo, x), head: 16 (over y, z_hi, core).
Axes of the slice: x: 4, y: 4, z: 4 (z_hi: 2, z_lo: 2; z = z_hi * 2 + z_lo), core: 2. Of those that a mesh axis runs over, the one named last changes fastest.
Arguments:
- tokens: float32 [16, 1024, 1024], P('frame', 'head'), may hold values from -48 to 48
- qkv_weight: float32 [1024, 3072], replicated
- out_weight: float32 [1024, 1024], replicated, may hold values from -0.1875 to 0.1875
- norm_gain: float32 [1024], replicated, may hold values from 0.1 to 1.9
- proj_weight: float32 [1024, 256], replicated, may hold values from -0.1875 to 0.1875
- up_weight: bfloat16 [256, 4096], replicated, may hold values from -0.375 to 0.375
- conv_weight: bfloat16 [2, 3, 3, 256, 256], replicated, may hold values from -0.125 to 0.125
- conv_bias: float32 [2, 256], replicated, may hold values from -3 to 3
- block_lists: int32 [128, 26], P('frame'), may hold values from 0 to 127, as said below
- block_counts: int32 [128], P('frame'), may hold values from 1 to 26, as said below
Outputs:
- refined: bfloat16 [16, 128, 128, 256], P('frame', 'head')
Inputs may be any that keep to these rules, and one draw needn't show every extreme that they name: `block_lists`: row b names 26 different key blocks and its first entry is block b itself; entries at or after the row's count are padding and are ignored. `block_counts`: some query block in every draw has all 26 entries valid.
All inputs are finite; a program needn't handle non-finite values.
Results may differ from a plain program's by a relative error of at most 0.0057.
Values may be sent and summed in bfloat16 or wider, within the bound.
No kernel may reach another device: no remote copies, remote signals or barrier semaphores. Data moves between devices by JAX's collectives and lax.ppermute only.
A program may use at most 128 MiB of HBM per device.

v0:
```python
import math

import jax
import jax.numpy as jnp
from jax import lax
from jax.sharding import PartitionSpec as P

HEADS = 16
GRID = 32
BLOCK = 128


highest = lax.Precision.HIGHEST
eps_norm = 1e-05


def extended_2(block, sides, width):
    for axis, dim in sides:
        count = lax.axis_size(axis)
        forward = [(i, i + 1) for i in range(count - 1)]
        backward = [(target, source) for source, target in forward]
        low = lax.ppermute(
            lax.slice_in_dim(block, block.shape[dim] - width, None, axis=dim), axis, forward
        )
        high = lax.ppermute(lax.slice_in_dim(block, 0, width, axis=dim), axis, backward)
        block = jnp.concatenate([low, block, high], axis=dim)
    return block


def attend_padded(queries, key_values, block_ids, counts, factor):
    groups, slot_total = block_ids.shape
    block_size = queries.shape[1]
    half = queries.shape[3] // 2
    picked = key_values[block_ids]
    picked = picked.reshape((groups, slot_total * block_size) + picked.shape[3:])
    scores = jnp.einsum("gihe,gjhe->ghij", queries, picked, precision=highest) * factor
    slot_of = jnp.arange(slot_total * block_size, dtype=jnp.int32) // block_size
    usable = slot_of[None, :] < counts[:, None]
    scores = jnp.where(usable[:, None, None, :], scores, -jnp.inf)
    row_max = jnp.max(scores, axis=3, keepdims=True)
    weights = jnp.exp(scores - row_max)
    totals = jnp.sum(weights, axis=3)
    blended = jnp.einsum("ghij,gjhe->gihe", weights, picked, precision=highest)
    return blended[:, :, :, half:] / jnp.transpose(totals, (0, 2, 1))[:, :, :, None]


def layer_norm(rows, gain):
    centre = jnp.mean(rows, axis=-1, keepdims=True)
    centred = rows - centre
    spread = jnp.mean(centred * centred, axis=-1, keepdims=True)
    return centred * lax.rsqrt(spread + eps_norm) * gain


def conv_window(padded, weight):
    frames_here, rows_in, cols_in, channels = padded.shape
    rows_out = rows_in - 2
    cols_out = cols_in - 2
    summed = jnp.zeros((frames_here * rows_out * cols_out, weight.shape[-1]), jnp.float32)
    for row_off in range(3):
        for col_off in range(3):
            window = padded[:, row_off : row_off + rows_out, col_off : col_off + cols_out, :]
            summed = summed + jnp.dot(
                window.reshape(-1, channels),
                weight[row_off, col_off],
                preferred_element_type=jnp.float32,
            )
    return summed.reshape(frames_here, rows_out, cols_out, -1)


def pad_columns(image):
    return jnp.pad(image, ((0, 0), (0, 0), (1, 1), (0, 0)))


def on_device(
    tokens,
    qkv_weight,
    out_weight,
    norm_gain,
    proj_weight,
    up_weight,
    conv_weight,
    conv_bias,
    block_lists,
    block_counts,
):
    local_frames, strip_tokens, model_width = tokens.shape
    head_groups = lax.axis_size("head")
    local_heads = HEADS // head_groups
    head_dim = model_width // HEADS
    column_width = local_heads * 3 * head_dim
    frame_tokens = strip_tokens * head_groups
    flat_strip = tokens.reshape(-1, model_width)
    packed = jnp.dot(flat_strip, qkv_weight, precision=highest, preferred_element_type=jnp.float32)
    packed = packed.reshape(local_frames, strip_tokens, head_groups, column_width)
    packed = lax.all_to_all(packed, "head", split_axis=2, concat_axis=1, tiled=True)
    local_rows = local_frames * frame_tokens
    packed = packed.reshape(local_rows, local_heads, 3 * head_dim)
    query_mask = (jnp.arange(2 * head_dim, dtype=jnp.int32) < head_dim).astype(jnp.float32)
    queries = (packed[:, :, : 2 * head_dim] * query_mask).reshape(
        -1, BLOCK, local_heads, 2 * head_dim
    )
    own_pairs = packed[:, :, head_dim:].reshape(local_rows, local_heads * 2 * head_dim)
    all_pairs = lax.all_gather(own_pairs, "frame", axis=0, tiled=True)
    all_pairs = all_pairs.reshape(-1, BLOCK, local_heads, 2 * head_dim)
    local_blocks = queries.shape[0]
    group_blocks = math.gcd(local_blocks, max(1, 512 // BLOCK))
    group_count = local_blocks // group_blocks
    factor = head_dim ** (-0.5)
    grouped = (
        queries.reshape(group_count, group_blocks, BLOCK, local_heads, 2 * head_dim),
        block_lists.reshape(group_count, group_blocks, -1),
        block_counts.reshape(group_count, group_blocks),
    )

    def one_group(items):
        return attend_padded(items[0], all_pairs, items[1], items[2], factor)

    attended = lax.map(one_group, grouped)
    attended = attended.reshape(local_frames, head_groups, strip_tokens, local_heads * head_dim)
    attended = lax.all_to_all(attended, "head", split_axis=1, concat_axis=3, tiled=True)
    attended = attended.reshape(-1, model_width)
    stream = flat_strip + jnp.dot(
        attended, out_weight, precision=highest, preferred_element_type=jnp.float32
    )
    normed = layer_norm(stream, norm_gain)
    features = jnp.dot(
        normed, proj_weight, precision=highest, preferred_element_type=jnp.float32
    ).astype(jnp.bfloat16)
    channels = features.shape[1]
    strip_rows = strip_tokens // GRID
    lifted = jnp.dot(features, up_weight, preferred_element_type=jnp.float32).astype(jnp.bfloat16)
    lifted = lifted.reshape(local_frames, strip_rows, GRID, 4, 4, channels)
    upsampled = jnp.transpose(lifted, (0, 1, 3, 2, 4, 5)).reshape(
        local_frames, 4 * strip_rows, 4 * GRID, channels
    )
    activated = jnp.maximum(upsampled, jnp.zeros((), jnp.bfloat16))
    pixel_rows = 4 * strip_rows
    deep_rim = extended_2(activated, (("head", 1),), 2)
    first_conv = conv_window(pad_columns(deep_rim), conv_weight[0]) + conv_bias[0]
    hidden = jnp.maximum(first_conv, 0.0).astype(jnp.bfloat16)
    position = lax.axis_index("head")
    row_ids = jnp.arange(pixel_rows + 2, dtype=jnp.int32)
    inside = ((row_ids > 0) | (position > 0)) & (
        (row_ids < pixel_rows + 1) | (position < head_groups - 1)
    )
    extended = jnp.where(inside[None, :, None, None], hidden, jnp.zeros((), jnp.bfloat16))
    second = conv_window(pad_columns(extended), conv_weight[1]) + conv_bias[1]
    return (upsampled.astype(jnp.float32) + second).astype(jnp.bfloat16)


def solution(mesh):
    in_specs = (
        P("frame", "head", None),
        P(),
        P(),
        P(),
        P(),
        P(),
        P(),
        P(),
        P("frame", None),
        P("frame"),
    )
    out_specs = P("frame", "head", None, None)
    return jax.shard_map(
        on_device, mesh=mesh, in_specs=in_specs, out_specs=out_specs, check_vma=False
    )
```

profile of v0, /device:TPU:1, one launch (start us, length us, event | category | flops | bytes accessed | tf_op | source)
XLA Modules:
  0.0 411.2 jit_solution(11181766817035255600)
XLA Ops:
  6.5 12.7 %copy.53 = f32[1024,3072]{0,1:T(8,128)} copy(f32[1024,3072]{1,0:T(8,128)} %param.13) | data formatting | bytes 25165824 | tf_op args[1]
  19.3 16.2 %fusion.13 = f32[2,64,16,192]{3,1,0,2:T(8,128)} fusion(f32[16,192,1024,1]{2,1,3,0:T(8,128)} %bitcast.188, f32[2,64,1024]{2,1,0:T(8,128)S(1)} %copy-done.4), kind=kOutput, calls=%fused_computation.59 | convolution fusion | flops 4831838208 | bytes 14680064 | tf_op jit(solution)/shard_map/dot_general | solution.py:93
  35.5 9.3 %all-to-all-start = ((f32[2,64,16,192]{3,1,0,2:T(8,128)}), f32[2,64,16,192]{3,1,0,2:T(8,128)}, u32[]{:S(2)}, u32[]{:S(2)}) async-start(f32[2,64,16,192]{3,1,0,2:T(8,128)} %fusion.13), calls=%async_computation | async-start | bytes 4194304 | tf_op jit(solution)/shard_map/all_to_all | solution.py:95
  44.8 28.4 %all-to-all-done = f32[2,64,16,192]{3,1,0,2:T(8,128)} async-done(((f32[2,64,16,192]{3,1,0,2:T(8,128)}), f32[2,64,16,192]{3,1,0,2:T(8,128)}, u32[]{:S(2)}, u32[]{:S(2)}) %all-to-all-start) | async-done | bytes 1572896 | tf_op jit(solution)/shard_map/all_to_all | solution.py:95
  76.5 91.5 %all-gather.3.cloned.1.call-done = f32[16384,1,128]{2,0,1:T(8,128)} async-done(((f32[2048,1,128]{2,0,1:T(8,128)}), f32[16384,1,128]{2,0,1:T(8,128)}) %all-gather.3.cloned.1.call-update) | async-done | bytes 8388624 | tf_op jit(solution)/shard_map/all_gather | solution.py:103
  168.0 137.8 %while.12 = (s32[]{:T(128)}, f32[4,4,128,1,64]{2,1,0,4,3:T(4,128)}, s32[4,4,26]{2,1,0:T(4,128)}, f32[128,128,1,128]{3,2,1,0:T(1,128)}, s32[4,4]{1,0:T(4,128)S(1)}, /*index=5*/f32[4,4,128,1,128]{4,2,1,3,0:T(8,128)S(1)}, s32[]{:T(128)}) while((s32[]{:T(128)}, f32[4,4,128,1,64]{2,1,0,4,3:T(4,128)}, s32[4,4,26]{2,1,0:T(4,128)}, ...), condition=%wide.region_3.4_spmd, body=%wide.region_0.3_spmd.sunk | while | flops 5244788224 | bytes 69276288 | solution.py:118
  180.2 7.2 %gather_fusion = f32[104,128,128]{2,1,0:T(8,128)} fusion(f32[128,128,128]{2,1,0:T(8,128)} %bitcast.187, s32[1024]{0:T(1024)S(1)} %pad_clamp_fusion.2), kind=kCustom, calls=%fused_computation.clone.1 | custom fusion | bytes 13631904 | tf_op jit(solution)/shard_map/while/body/eval_jaxpr/gather | solution.py:34
  187.5 9.7 %fusion.63 = (f32[4,128]{1,0:T(4,128)S(1)}, f32[4,128,3328]{2,1,0:T(8,128)S(1)}) fusion(f32[4,3328,128]{2,1,0:T(8,128)} %bitcast.182, f32[4,4,128,1,128]{4,2,1,3,0:T(8,128)S(1)} %get-tuple-element.194, s32[]{:T(128)S(6)} %copy.88, pred[4,3328]{1,0:T(4,128)(4,1)S(1)} %broadcast_compare_fusion.2), kind=kOutput, calls=%fused_computation.99.clone.1 | convolution fusion | flops 2622356992 | bytes 13908996 | tf_op jit(solution)/shard_map/while/body/eval_jaxpr/gihe,gjhe->ghij/dot_general | solution.py:36
  197.3 11.7 %fusion.64 = f32[4,128,1,128]{1,3,0,2:T(8,128)S(1)} fusion(f32[4,3328,128]{2,1,0:T(8,128)S(1)} %bitcast.185, f32[4,128,3328]{2,1,0:T(8,128)S(1)} %get-tuple-element.173, f32[4,128]{1,0:T(4,128)S(1)} %get-tuple-element.174), kind=kOutput, calls=%fused_computation.6.clone.1 | convolution fusion | flops 2618949632 | bytes 13895680 | tf_op jit(solution)/shard_map/while/body/eval_jaxpr/ghij,gjhe->gihe/dot_general | solution.py:43
  211.7 7.2 %gather_fusion = f32[104,128,128]{2,1,0:T(8,128)} fusion(f32[128,128,128]{2,1,0:T(8,128)} %bitcast.187, s32[1024]{0:T(1024)S(1)} %pad_clamp_fusion.2), kind=kCustom, calls=%fused_computation.clone.1 | custom fusion | bytes 13631904 | tf_op jit(solution)/shard_map/while/body/eval_jaxpr/gather | solution.py:34
  219.0 9.7 %fusion.63 = (f32[4,128]{1,0:T(4,128)S(1)}, f32[4,128,3328]{2,1,0:T(8,128)S(1)}) fusion(f32[4,3328,128]{2,1,0:T(8,128)} %bitcast.182, f32[4,4,128,1,128]{4,2,1,3,0:T(8,128)S(1)} %get-tuple-element.194, s32[]{:T(128)S(6)} %copy.88, pred[4,3328]{1,0:T(4,128)(4,1)S(1)} %broadcast_compare_fusion.2), kind=kOutput, calls=%fused_computation.99.clone.1 | convolution fusion | flops 2622356992 | bytes 13908996 | tf_op jit(solution)/shard_map/while/body/eval_jaxpr/gihe,gjhe->ghij/dot_general | solution.py:36
  228.8 11.7 %fusion.64 = f32[4,128,1,128]{1,3,0,2:T(8,128)S(1)} fusion(f32[4,3328,128]{2,1,0:T(8,128)S(1)} %bitcast.185, f32[4,128,3328]{2,1,0:T(8,128)S(1)} %get-tuple-element.173, f32[4,128]{1,0:T(4,128)S(1)} %get-tuple-element.174), kind=kOutput, calls=%fused_computation.6.clone.1 | convolution fusion | flops 2618949632 | bytes 13895680 | tf_op jit(solution)/shard_map/while/body/eval_jaxpr/ghij,gjhe->gihe/dot_general | solution.py:43
  243.1 7.2 %gather_fusion = f32[104,128,128]{2,1,0:T(8,128)} fusion(f32[128,128,128]{2,1,0:T(8,128)} %bitcast.187, s32[1024]{0:T(1024)S(1)} %pad_clamp_fusion.2), kind=kCustom, calls=%fused_computation.clone.1 | custom fusion | bytes 13631904 | tf_op jit(solution)/shard_map/while/body/eval_jaxpr/gather | solution.py:34
  250.5 9.7 %fusion.63 = (f32[4,128]{1,0:T(4,128)S(1)}, f32[4,128,3328]{2,1,0:T(8,128)S(1)}) fusion(f32[4,3328,128]{2,1,0:T(8,128)} %bitcast.182, f32[4,4,128,1,128]{4,2,1,3,0:T(8,128)S(1)} %get-tuple-element.194, s32[]{:T(128)S(6)} %copy.88, pred[4,3328]{1,0:T(4,128)(4,1)S(1)} %broadcast_compare_fusion.2), kind=kOutput, calls=%fused_computation.99.clone.1 | convolution fusion | flops 2622356992 | bytes 13908996 | tf_op jit(solution)/shard_map/while/body/eval_jaxpr/gihe,gjhe->ghij/dot_general | solution.py:36
  260.3 11.7 %fusion.64 = f32[4,128,1,128]{1,3,0,2:T(8,128)S(1)} fusion(f32[4,3328,128]{2,1,0:T(8,128)S(1)} %bitcast.185, f32[4,128,3328]{2,1,0:T(8,128)S(1)} %get-tuple-element.173, f32[4,128]{1,0:T(4,128)S(1)} %get-tuple-element.174), kind=kOutput, calls=%fused_computation.6.clone.1 | convolution fusion | flops 2618949632 | bytes 13895680 | tf_op jit(solution)/shard_map/while/body/eval_jaxpr/ghij,gjhe->gihe/dot_general | solution.py:43
  274.6 7.2 %gather_fusion = f32[104,128,128]{2,1,0:T(8,128)} fusion(f32[128,128,128]{2,1,0:T(8,128)} %bitcast.187, s32[1024]{0:T(1024)S(1)} %pad_clamp_fusion.2), kind=kCustom, calls=%fused_computation.clone.1 | custom fusion | bytes 13631904 | tf_op jit(solution)/shard_map/while/body/eval_jaxpr/gather | solution.py:34
  282.0 9.7 %fusion.63 = (f32[4,128]{1,0:T(4,128)S(1)}, f32[4,128,3328]{2,1,0:T(8,128)S(1)}) fusion(f32[4,3328,128]{2,1,0:T(8,128)} %bitcast.182, f32[4,4,128,1,128]{4,2,1,3,0:T(8,128)S(1)} %get-tuple-element.194, s32[]{:T(128)S(6)} %copy.88, pred[4,3328]{1,0:T(4,128)(4,1)S(1)} %broadcast_compare_fusion.2), kind=kOutput, calls=%fused_computation.99.clone.1 | convolution fusion | flops 2622356992 | bytes 13908996 | tf_op jit(solution)/shard_map/while/body/eval_jaxpr/gihe,gjhe->ghij/dot_general | solution.py:36
  291.8 11.7 %fusion.64 = f32[4,128,1,128]{1,3,0,2:T(8,128)S(1)} fusion(f32[4,3328,128]{2,1,0:T(8,128)S(1)} %bitcast.185, f32[4,128,3328]{2,1,0:T(8,128)S(1)} %get-tuple-element.173, f32[4,128]{1,0:T(4,128)S(1)} %get-tuple-element.174), kind=kOutput, calls=%fused_computation.6.clone.1 | convolution fusion | flops 2618949632 | bytes 13895680 | tf_op jit(solution)/shard_map/while/body/eval_jaxpr/ghij,gjhe->gihe/dot_general | solution.py:43
  311.8 7.4 %all-to-all-start.1 = ((f32[16,1,8192]{2,1,0:T(1,128)}), f32[16,1,8192]{2,1,0:T(1,128)S(1)}, u32[]{:S(2)}, u32[]{:S(2)}) async-start(f32[16,1,8192]{2,1,0:T(1,128)} %reshape.300), calls=%async_computation.1 | async-start | bytes 1048576 | tf_op jit(solution)/shard_map/all_to_all | solution.py:120
  322.5 7.9 %all-to-all-done.1 = f32[16,1,8192]{2,1,0:T(1,128)S(1)} async-done(((f32[16,1,8192]{2,1,0:T(1,128)}), f32[16,1,8192]{2,1,0:T(1,128)S(1)}, u32[]{:S(2)}, u32[]{:S(2)}) %all-to-all-start.1) | async-done | bytes 524320 | tf_op jit(solution)/shard_map/all_to_all | solution.py:120
  338.6 4.9 %fusion.26 = (f32[128]{0:T(128)S(1)}, f32[128,1024]{1,0:T(8,128)S(1)}) fusion(f32[128,1024]{1,0:T(8,128)} %bitcast.216, f32[128,1024]{0,1:T(8,128)S(1)} %reshape.299, f32[1024,1024]{1,0:T(8,128)} %param.14), kind=kOutput, calls=%fused_computation.102 | convolution fusion | flops 1610874752 | bytes 5767680 | tf_op jit(solution)/shard_map/dot_general | solution.py:122
  372.2 8.2 %pad_slice_fusion.6 = (bf16[2,10,128,256]{3,0,2,1:T(2,128)(2,1)S(1)}, bf16[2,10,128,256]{3,0,2,1:T(2,128)(2,1)S(1)}, bf16[2,10,128,256]{3,0,2,1:T(2,128)(2,1)S(1...) fusion(bf16[2,12,128,256]{3,0,2,1:T(2,128)(2,1)S(1)} %pad_maxim, ...), kind=kLoop, calls=%fused_computation.93 | loop fusion | bytes 12058624 | tf_op jit(solution)/shard_map/slice | solution.py:61
  380.6 4.4 %pad_maximum_fusion.2 = (bf16[2,10,128,256]{3,0,2,1:T(2,128)(2,1)S(1)}, bf16[2,10,128,256]{3,0,2,1:T(2,128)(2,1)S(1)}) fusion(bf16[2,2,128,256]{3,0,2,1:T(2,128)(2,1)S(1)} %collective-permute-done.1, bf16[2,8,128,256]{3,0,2,1:T(2,128)(2,1)S(1)} %bitcast.191, bf16[2,2,128,256]{3,0,2,1:T(2,128)(2,1)} %collective-permute-done), kind=kLoop, calls=%fused_computation.47 | loop fusion | flops 1310720 | bytes 4194304 | tf_op jit(solution)/shard_map/concatenate | solution.py:26
  393.2 4.3 %pad_slice_fusion = (bf16[2,8,128,256]{3,2,1,0:T(8,128)(2,1)S(1)}, bf16[2,8,128,256]{3,2,1,0:T(8,128)(2,1)S(1)}, bf16[2,8,128,256]{3,2,1,0:T(8,128)(2,1)S(1)}, b...) fusion(bf16[2,10,128,256]{3,2,1,0:T(8,128)(2,1)S(1)} %fusion.12), kind=kLoop, calls=%fused_computation.53 | loop fusion | bytes 13893632 | tf_op jit(solution)/shard_map/slice | solution.py:61
  (137 shorter events, 75.0 us)
Async XLA Ops:
  6.5 337.9 %copy-start = (bf16[256,4096]{1,0:T(8,128)(2,1)S(1)}, bf16[256,4096]{1,0:T(8,128)(2,1)}, u32[]{:S(2)}) copy-start(bf16[256,4096]{1,0:T(8,128)(2,1)} %param.17) | copy-start | bytes 6291460
  6.5 12.7 %copy-start.4 = (f32[2,64,1024]{2,1,0:T(8,128)S(1)}, f32[2,64,1024]{2,1,0:T(8,128)}, u32[]{:S(2)}) copy-start(f32[2,64,1024]{2,1,0:T(8,128)} %param.12) | copy-start | bytes 1572868
  35.5 37.7 %all-to-all-start = ((f32[2,64,16,192]{3,1,0,2:T(8,128)}), f32[2,64,16,192]{3,1,0,2:T(8,128)}, u32[]{:S(2)}, u32[]{:S(2)}) async-start(f32[2,64,16,192]{3,1,0,2:T(8,128)} %fusion.13), calls=%async_computation | async-start | bytes 4194304 | tf_op jit(solution)/shard_map/all_to_all | solution.py:95
  44.8 123.2 %all-gather.3.cloned.1.call-start = ((), (), s32[]{:S(2)}) async-start(), calls=%async_computation.2 | async-start | bytes 9437184 | tf_op jit(solution)/shard_map/all_gather | solution.py:103
  75.0 1.4 copy-start.8
  187.4 9.9 %slice-start = ((s8[6815744]{0:T(1024)(128)(4,1)}), s8[4194304]{0:T(1024)(128)(4,1)S(1)}, s32[]{:S(2)}) async-start(s8[6815744]{0:T(1024)(128)(4,1)} %bitcast.183), calls=%async_computation.3 | async-start | bytes 8388608 | tf_op jit(solution)/shard_map/while
  187.5 9.8 %slice-start.1 = ((s8[6815744]{0:T(1024)(128)(4,1)}), s8[2621440]{0:T(1024)(128)(4,1)S(1)}, s32[]{:S(2)}) async-start(s8[6815744]{0:T(1024)(128)(4,1)} %bitcast.183), calls=%async_computation.4 | async-start | bytes 5242880 | tf_op jit(solution)/shard_map/while
  218.9 9.9 %slice-start = ((s8[6815744]{0:T(1024)(128)(4,1)}), s8[4194304]{0:T(1024)(128)(4,1)S(1)}, s32[]{:S(2)}) async-start(s8[6815744]{0:T(1024)(128)(4,1)} %bitcast.183), calls=%async_computation.3 | async-start | bytes 8388608 | tf_op jit(solution)/shard_map/while
  219.0 9.8 %slice-start.1 = ((s8[6815744]{0:T(1024)(128)(4,1)}), s8[2621440]{0:T(1024)(128)(4,1)S(1)}, s32[]{:S(2)}) async-start(s8[6815744]{0:T(1024)(128)(4,1)} %bitcast.183), calls=%async_computation.4 | async-start | bytes 5242880 | tf_op jit(solution)/shard_map/while
  250.4 9.9 %slice-start = ((s8[6815744]{0:T(1024)(128)(4,1)}), s8[4194304]{0:T(1024)(128)(4,1)S(1)}, s32[]{:S(2)}) async-start(s8[6815744]{0:T(1024)(128)(4,1)} %bitcast.183), calls=%async_computation.3 | async-start | bytes 8388608 | tf_op jit(solution)/shard_map/while
  250.5 9.8 %slice-start.1 = ((s8[6815744]{0:T(1024)(128)(4,1)}), s8[2621440]{0:T(1024)(128)(4,1)S(1)}, s32[]{:S(2)}) async-start(s8[6815744]{0:T(1024)(128)(4,1)} %bitcast.183), calls=%async_computation.4 | async-start | bytes 5242880 | tf_op jit(solution)/shard_map/while
  281.9 9.9 %slice-start = ((s8[6815744]{0:T(1024)(128)(4,1)}), s8[4194304]{0:T(1024)(128)(4,1)S(1)}, s32[]{:S(2)}) async-start(s8[6815744]{0:T(1024)(128)(4,1)} %bitcast.183), calls=%async_computation.3 | async-start | bytes 8388608 | tf_op jit(solution)/shard_map/while
  282.0 9.8 %slice-start.1 = ((s8[6815744]{0:T(1024)(128)(4,1)}), s8[2621440]{0:T(1024)(128)(4,1)S(1)}, s32[]{:S(2)}) async-start(s8[6815744]{0:T(1024)(128)(4,1)} %bitcast.183), calls=%async_computation.4 | async-start | bytes 5242880 | tf_op jit(solution)/shard_map/while
  311.8 18.6 %all-to-all-start.1 = ((f32[16,1,8192]{2,1,0:T(1,128)}), f32[16,1,8192]{2,1,0:T(1,128)S(1)}, u32[]{:S(2)}, u32[]{:S(2)}) async-start(f32[16,1,8192]{2,1,0:T(1,128)} %reshape.300), calls=%async_computation.1 | async-start | bytes 1048576 | tf_op jit(solution)/shard_map/all_to_all | solution.py:120
  338.5 5.1 %copy-start.5 = (f32[1024,256]{1,0:T(8,128)S(1)}, f32[1024,256]{1,0:T(8,128)}, u32[]{:S(2)}) copy-start(f32[1024,256]{1,0:T(8,128)} %param.16) | copy-start | bytes 3145732
  338.6 5.1 %copy-start.6 = (f32[1024]{0:T(1024)S(1)}, f32[1024]{0:T(1024)}, u32[]{:S(2)}) copy-start(f32[1024]{0:T(1024)} %param.15) | copy-start | bytes 12292
  347.4 11.1 %copy-start.7 = (f32[2,256]{1,0:T(2,128)S(1)}, f32[2,256]{1,0:T(2,128)}, u32[]{:S(2)}) copy-start(f32[2,256]{1,0:T(2,128)} %param.19) | copy-start | bytes 6148
  351.5 17.4 %collective-permute-start.1 = (bf16[2,2,128,256]{3,0,2,1:T(2,128)(2,1)}, bf16[2,2,128,256]{3,0,2,1:T(2,128)(2,1)S(1)}, u32[]{:S(2)}, u32[]{:S(2)}) collective-permute-start(bf16[2,2,128,256]{3,0,2,1:T(2,128)(2,1)} %get-tuple-element.127), channel_id=1, source_target_pairs={{1,0},{2,1},{3,2},{4,3},{5,4},{6,5},{7,6},{8,7},{9,8},{10,9},{11,1... | collective-permute-start | bytes 786440 | tf_op jit(solution)/shard_map/ppermute | solution.py:25
  354.6 14.3 %collective-permute-start = (bf16[2,2,128,256]{3,0,2,1:T(2,128)(2,1)}, bf16[2,2,128,256]{3,0,2,1:T(2,128)(2,1)}, u32[]{:S(2)}, u32[]{:S(2)}) collective-permute-start(bf16[2,2,128,256]{3,0,2,1:T(2,128)(2,1)} %get-tuple-element.126), channel_id=1, source_target_pairs={{0,1},{1,2},{2,3},{3,4},{4,5},{5,6},{6,7},{7,8},{8,9},{9,10},{10,1... | collective-permute-start | bytes 786440 | tf_op jit(solution)/shard_map/ppermute | solution.py:22
  386.4 1.3 copy-start.2
  393.2 4.3 %copy-start.3 = (bf16[3,3,256,256]{3,2,1,0:T(8,128)(2,1)S(1)}, bf16[3,3,256,256]{3,2,1,0:T(8,128)(2,1)}, u32[]{:S(2)}) copy-start(bf16[3,3,256,256]{3,2,1,0:T(8,128)(2,1)} %get-tuple-element.104) | copy-start | bytes 3538948
  401.2 1.6 copy-start.1
Sparse Core Ops, SparseCore 0:
  76.5 91.4 all-gather.2
where the time goes:
time: 417 us; the launch traced here: 411 us
  waiting for transfers between devices  128 us (31%)
  matrix products  118 us (28%)
  local copies, waits for them, and re-layouts  93.9 us (23%)
  starting transfers between devices  23.8 us (6%)
  other arithmetic  21.6 us (5%)
  between operations  14 us (3%)
  loops' own time  12 us (3%)
    all_gather x1, waiting for transfers between devices, on_device(): all_pairs = lax.all_gather(own_pairs, 'frame', axis=0, tiled=True)  91.5 us
    dot_general x4, matrix products, attend_padded(): blended = jnp.einsum('ghij,gjhe->gihe', weights, picked, precision=highest)  47 us
    dot_general x4, matrix products, attend_padded(): jnp.einsum('gihe,gjhe->ghij', queries, picked, precision=highest) * factor  39 us
    gather x4, local copies, waits for them, and re-layouts, attend_padded(): picked = key_values[block_ids]  28.9 us
    all_to_all x1, waiting for transfers between devices, on_device(): lax.all_to_all(packed, 'head', split_axis=2, concat_axis=1, tiled=True)  28.4 us
    unnamed x21, local copies, waits for them, and re-layouts  19.6 us
    dot_general x1, matrix products, on_device(): jnp.dot(flat_strip, qkv_weight, precision=highest, preferred_element_type...  16.2 us
    slice x9, local copies, waits for them, and re-layouts, conv_window(): padded[:, row_off:row_off + rows_out, col_off:col_off + cols_out, :]  14 us
  transfers between devices with their start and end apart: 5, of which 3 were waited for; matrix products, arithmetic and copies ran while one was open for 3% of the time, Pallas kernels for 0%

commit v1 on v0

v1 whole, which is shorter than its diff:
```python
import jax
import jax.numpy as jnp
from jax import lax
from jax.experimental import pallas as pl
from jax.experimental.pallas import tpu as pltpu
from jax.sharding import Mesh, PartitionSpec as P

D = 1024
HEADS = 16
HD = 64
CH = 256
SLOTS = 26
STRIP = 64
NEG = -2e38
bf16 = jnp.bfloat16
f32 = jnp.float32


def split(v):
    hi = v.astype(bf16)
    return hi, (v - hi.astype(f32)).astype(bf16)


def dot(a, b):
    return jnp.dot(a, b, preferred_element_type=f32)


def dot3(ah, al, bh, bl):
    return dot(ah, bh) + (dot(al, bh) + dot(ah, bl))


def lanes(shape):
    return lax.broadcasted_iota(jnp.int32, shape, len(shape) - 1)


def qkv_body(x_ref, w_ref, out_ref, xh, xl):
    @pl.when(pl.program_id(0) == 0)
    def _():
        hi, lo = split(x_ref[...])
        xh[...] = hi
        xl[...] = lo

    wh, wl = split(w_ref[...])
    r = dot3(xh[...], xl[...], wh, wl)
    for u in range(2):
        q = r[:, u * 192 : u * 192 + HD] * 0.125
        k = r[:, u * 192 + HD : u * 192 + 2 * HD]
        v = r[:, u * 192 + 2 * HD : u * 192 + 3 * HD]
        for i, t in enumerate((q, k)):
            lo = t - t.astype(bf16).astype(f32)
            out_ref[u, i * 128 : i * 128 + 128, :] = jnp.concatenate([t, lo], axis=1).astype(bf16)
        out_ref[u, 256:320, :] = jnp.concatenate([v[:STRIP], v[STRIP:]], axis=1).astype(bf16)


def qkv(x, w):
    return pl.pallas_call(
        qkv_body,
        grid=(HEADS // 2,),
        in_specs=[
            pl.BlockSpec((128, D), lambda g: (0, 0)),
            pl.BlockSpec((D, 384), lambda g: (0, g)),
        ],
        out_specs=pl.BlockSpec((2, 320, 128), lambda g: (g, 0, 0)),
        out_shape=jax.ShapeDtypeStruct((HEADS, 320, 128), bf16),
        scratch_shapes=[pltpu.VMEM((128, D), bf16), pltpu.VMEM((128, D), bf16)],
        name="qkv",
    )(x, w)


GROUP = 4


def attend_body(ids, cnt, info, kv0, kv1, q0, q1, q2, q3, o_ref, ks, vs, res, ms, accs):
    low = lanes((128, 128)) < HD
    for src, kv in enumerate((kv0, kv1)):

        def keys(j, _):
            for fr in range(2):
                b = src * 16 + fr * 8 + j
                a = jnp.concatenate(
                    [kv[2 * j, fr * 64 : fr * 64 + 64, :], kv[2 * j + 1, fr * 64 : fr * 64 + 64, :]],
                    axis=0,
                )
                ks[b, :, 0:128] = a
                ks[b, :, 128:256] = pltpu.roll(a.astype(f32), 64, 1).astype(bf16)
                v = jnp.concatenate([kv[2 * j, 128:192, :], kv[2 * j + 1, 128:192, :]], axis=0)
                v = v.astype(f32)
                if fr:
                    v = pltpu.roll(v, 64, 1)
                vs[b] = jnp.where(low, v, 1.0).astype(bf16)
            return 0

        lax.fori_loop(0, 8, keys, 0)

    for s, q in enumerate((q0, q1, q2, q3)):

        def group(g, _):
            fr = g // 2
            j0 = (g % 2) * GROUP
            first = s * 16 + g * GROUP
            most = cnt[first]
            for u in range(1, GROUP):
                most = jnp.maximum(most, cnt[first + u])
            trips = jnp.maximum((most + 1) // 2, 1)
            row = pl.multiple_of(fr * 64, 64)
            qs = []
            for u in range(GROUP):
                j = j0 + u
                a = jnp.concatenate(
                    [q[2 * j, pl.ds(row, 64), :], q[2 * j + 1, pl.ds(row, 64), :]], axis=0
                )
                qs.append(jnp.concatenate([a, a], axis=1))
                ms[u] = jnp.full((128, 128), NEG, f32)
                accs[u] = jnp.zeros((128, 128), f32)

            def step(t, _):
                for u in range(GROUP):
                    b = first + u
                    ia = ids[b, 2 * t]
                    ib = ids[b, 2 * t + 1]
                    kk = jnp.concatenate([ks[ia], ks[ib]], axis=0)
                    vv = jnp.concatenate([vs[ia], vs[ib]], axis=0)
                    sc = lax.dot_general(
                        qs[u], kk, (((1,), (1,)), ((), ())), preferred_element_type=f32
                    )
                    sa = jnp.where(2 * t < cnt[b], sc[:, :128], NEG)
                    sb = jnp.where(2 * t + 1 < cnt[b], sc[:, 128:], NEG)
                    old = ms[u]
                    new = jnp.maximum(old, jnp.max(jnp.maximum(sa, sb), axis=1, keepdims=True))
                    p = jnp.concatenate([jnp.exp(sa - new), jnp.exp(sb - new)], axis=1)
                    accs[u] = accs[u] * jnp.exp(old - new) + dot(p.astype(bf16), vv)
                    ms[u] = new
                return 0

            lax.fori_loop(0, trips, step, 0)
            for u in range(GROUP):
                acc = accs[u]
                total = jnp.where(low, pltpu.roll(acc, 64, 1), acc)
                res[fr * 8 + j0 + u] = jnp.where(low, acc / total, ms[u] + jnp.log(total))
            return 0

        lax.fori_loop(0, 4, group, 0)
        to = info[s]

        def emit(j, _):
            r0 = res[j]
            r1 = res[8 + j]
            out = jnp.where(low, r0, pltpu.roll(r1, 64, 1)).astype(bf16)
            t0 = r0.T[HD : HD + 1, :]
            t1 = r1.T[HD : HD + 1, :]
            sub = lax.broadcasted_iota(jnp.int32, (16, 128), 0)
            for half in range(2):
                o_ref[to, 2 * j + half, 0:64, :] = out[half * 64 : half * 64 + 64]
                c = half * 64
                row = jnp.concatenate([t0[:, c : c + 64], t1[:, c : c + 64]], axis=1)
                hi = row.astype(bf16).astype(f32)
                mid = (row - hi).astype(bf16).astype(f32)
                last = row - hi - mid
                tile = jnp.where(sub == 0, hi, jnp.where(sub == 1, mid, jnp.where(sub == 2, last, 0.0)))
                o_ref[to, 2 * j + half, 64:80, :] = tile.astype(bf16)
            return 0

        lax.fori_loop(0, 8, emit, 0)


def attend(ids, cnt, info, kv0, kv1, qs):
    smem = pl.BlockSpec(memory_space=pltpu.SMEM)
    vmem = pl.BlockSpec(memory_space=pltpu.VMEM)
    return pl.pallas_call(
        attend_body,
        in_specs=[smem, smem, smem] + [vmem] * 6,
        out_specs=vmem,
        out_shape=jax.ShapeDtypeStruct((4, HEADS, 80, 128), bf16),
        scratch_shapes=[
            pltpu.VMEM((32, 128, 256), bf16),
            pltpu.VMEM((32, 128, 128), bf16),
            pltpu.VMEM((16, 128, 128), f32),
            pltpu.VMEM((GROUP, 128, 128), f32),
            pltpu.VMEM((GROUP, 128, 128), f32),
        ],
        name="attend",
    )(ids, cnt, info, kv0, kv1, *qs)


def mix_body(r_ref, x_ref, w_ref, gain_ref, proj_ref, feat_ref, top_ref, bot_ref, att):
    lse = jnp.sum(r_ref[:, 64:80, :].astype(f32), axis=1)
    parts = [lse[16 * x : 16 * x + 16] for x in range(4)]
    peak = jnp.maximum(jnp.maximum(parts[0], parts[1]), jnp.maximum(parts[2], parts[3]))
    es = [jnp.exp(p - peak) for p in parts]
    total = (es[0] + es[1]) + (es[2] + es[3])
    share = jnp.concatenate([e / total for e in es], axis=0)
    share = jnp.concatenate([share, share], axis=0).T
    both = jnp.where(lanes((STRIP, 128)) < 64, share[:STRIP], share[STRIP:])
    bh, bl = split(both)
    low = lanes((STRIP, 128)) < HD
    row = lax.broadcasted_iota(jnp.int32, (128, 2048), 0)
    col = lanes((128, 2048))
    half = ((row >= 64) == (col % 128 >= 64)) & True
    wide = []
    for x in range(4):
        spread = jnp.where(half & (row % 64 == 16 * x + col // 128), 1.0, 0.0).astype(bf16)
        wide.append(dot(bh, spread) + dot(bl, spread))
    for p in range(HEADS // 2):
        t = []
        for h in (2 * p, 2 * p + 1):
            acc = None
            for x in range(4):
                o = r_ref[16 * x + h, 0:64, :].astype(f32) * wide[x][:, 128 * h : 128 * h + 128]
                acc = o if acc is None else acc + o
            t.append(acc)
        att[0:64, 128 * p : 128 * p + 128] = jnp.where(low, t[0], pltpu.roll(t[1], 64, 1))
        att[64:128, 128 * p : 128 * p + 128] = jnp.where(low, pltpu.roll(t[0], 64, 1), t[1])
    ah, al = split(att[...])
    wh, wl = split(w_ref[...])
    stream = x_ref[...] + dot3(ah, al, wh, wl)
    centred = stream - jnp.mean(stream, axis=1, keepdims=True)
    spread = jnp.mean(centred * centred, axis=1, keepdims=True)
    normed = centred * lax.rsqrt(spread + 1e-05) * gain_ref[...]
    nh, nl = split(normed)
    ph, plo = split(proj_ref[...])
    feat = dot3(nh, nl, ph, plo).astype(bf16)
    feat_ref[...] = feat
    for f in range(2):
        top_ref[32 * f : 32 * f + 32] = feat[64 * f : 64 * f + 32]
        bot_ref[32 * f : 32 * f + 32] = feat[64 * f + 32 : 64 * f + 64]


def mix(r, x, w, gain, proj):
    return pl.pallas_call(
        mix_body,
        out_shape=(
            jax.ShapeDtypeStruct((128, CH), bf16),
            jax.ShapeDtypeStruct((64, CH), bf16),
            jax.ShapeDtypeStruct((64, CH), bf16),
        ),
        scratch_shapes=[pltpu.VMEM((128, D), f32)],
        name="mix",
    )(r, x, w, gain, proj)


def shifted(dst, src, rows, relu):
    def one(r, _):
        for dx in range(3):
            for half in range(2):
                v = src[half * rows + r, pl.ds(7 + dx, 128), :]
                if relu:
                    v = jnp.maximum(v, 0.0)
                dst[r, :, dx * 256 + half * 128 : dx * 256 + half * 128 + 128] = v.astype(bf16)
        return 0

    lax.fori_loop(0, rows, one, 0)


def head_body(pos, feat_ref, above_ref, below_ref, up_ref, cw_ref, cb_ref, out_ref, ups, u3, hid, h3):
    at = pos[0]

    @pl.when(pl.program_id(0) == 0)
    def _():
        for ref, rows in ((ups, 24), (hid, 20)):
            ref[:, 0:8, :] = jnp.zeros((rows, 8, 128), f32)
            ref[:, 136:144, :] = jnp.zeros((rows, 8, 128), f32)

    own = feat_ref[...]
    early = jnp.concatenate([own, below_ref[...]], axis=0)
    late = jnp.concatenate([above_ref[...], own], axis=0)
    for a in range(4):
        src = early if a < 2 else late
        lifted = dot(src, up_ref[:, 1024 * a : 1024 * a + 1024]).astype(bf16).astype(f32)
        for i in range(3):
            row = 2 + 4 * i + a if a < 2 else 4 * i + a - 2
            for e in range(4):
                for half in range(2):
                    c = 256 * e + 128 * half
                    ups[12 * half + row, pl.ds(8 + e, 32, stride=4), :] = lifted[
                        32 * i : 32 * i + 32, c : c + 128
                    ]
    shifted(u3, ups, 12, True)

    def conv1(r, _):
        acc = None
        for dy in range(3):
            part = dot(u3[pl.ds(2 * r + dy, 2)].reshape(256, 768), cw_ref[0, dy])
            acc = part if acc is None else acc + part
        h = jnp.maximum(acc + cb_ref[0:1, :], 0.0).astype(bf16).astype(f32)
        for k in range(2):
            y = 2 * r + k
            keep = ((y > 0) | (at > 0)) & ((y < 9) | (at < 15))
            v = jnp.where(keep, h[128 * k : 128 * k + 128], 0.0)
            for half in range(2):
                hid[10 * half + y, 8:136, :] = v[:, 128 * half : 128 * half + 128]
        return 0

    lax.fori_loop(0, 5, conv1, 0)
    shifted(h3, hid, 10, False)

    def conv2(r, _):
        acc = None
        for dy in range(3):
            part = dot(h3[pl.ds(2 * r + dy, 2)].reshape(256, 768), cw_ref[1, dy])
            acc = part if acc is None else acc + part
        acc = acc + cb_ref[1:2, :]
        for k in range(2):
            y = 2 * r + k
            for half in range(2):
                c = 128 * half
                v = ups[12 * half + y + 2, 8:136, :] + acc[128 * k : 128 * k + 128, c : c + 128]
                out_ref[0, y, :, c : c + 128] = v.astype(bf16)
        return 0

    lax.fori_loop(0, 4, conv2, 0)


def dense_head(pos, feat, above, below, up, cw, cb):
    whole = lambda shape: pl.BlockSpec(shape, lambda f: (0,) * len(shape))
    return pl.pallas_call(
        head_body,
        grid=(2,),
        in_specs=[
            pl.BlockSpec(memory_space=pltpu.SMEM),
            pl.BlockSpec((64, CH), lambda f: (f, 0)),
            pl.BlockSpec((32, CH), lambda f: (f, 0)),
            pl.BlockSpec((32, CH), lambda f: (f, 0)),
            whole((CH, 16 * CH)),
            whole((2, 3, 3 * CH, CH)),
            whole((2, CH)),
        ],
        out_specs=pl.BlockSpec((1, 8, 128, CH), lambda f: (f, 0, 0, 0)),
        out_shape=jax.ShapeDtypeStruct((2, 8, 128, CH), bf16),
        scratch_shapes=[
            pltpu.VMEM((24, 144, 128), f32),
            pltpu.VMEM((12, 128, 768), bf16),
            pltpu.VMEM((20, 144, 128), f32),
            pltpu.VMEM((10, 128, 768), bf16),
        ],
        name="dense_head",
    )(pos, feat, above, below, up, cw, cb)


def local_lists(lists, counts, x, z):
    packed = jnp.concatenate([lists, counts[:, None]], axis=1)
    sets = [packed] + [
        lax.ppermute(packed, "x", [(i, (i + k) % 4) for i in range(4)]) for k in (1, 2, 3)
    ]
    packed = jnp.concatenate(sets, axis=0)
    ids = packed[:, :SLOTS]
    slot = jnp.arange(SLOTS, dtype=jnp.int32)
    mine = (slot[None, :] < packed[:, SLOTS:]) & ((ids // 16) % 4 == x)
    local = jnp.where(ids // 64 == z, 0, 16) + ids % 16
    before = jnp.sum(
        jnp.where(mine[:, None, :] & (slot[None, None, :] < slot[None, :, None]), 1, 0), axis=2
    )
    place = mine[:, None, :] & (before[:, None, :] == slot[None, :, None])
    ids = jnp.sum(jnp.where(place, local[:, None, :], 0), axis=2)
    return ids.astype(jnp.int32), jnp.sum(mine, axis=1).astype(jnp.int32)


def on_device(tokens, qkv_w, out_w, gain, proj_w, up_w, conv_w, conv_b, lists, counts):
    x = lax.axis_index("x")
    z = lax.axis_index("z")
    strip = lax.axis_index("head")
    flat = tokens.reshape(-1, D)
    ids, cnt = local_lists(lists, counts, x, z)
    packed = qkv(flat, qkv_w)
    packed = lax.all_to_all(packed, "head", split_axis=0, concat_axis=0, tiled=True)
    q = packed[:, :128]
    kv = packed[:, 128:]
    kv_far = lax.ppermute(kv, "z", [(0, 1), (1, 0)])
    qs = [q] + [lax.ppermute(q, "x", [(i, (i + k) % 4) for i in range(4)]) for k in (1, 2, 3)]
    info = (x - jnp.arange(4, dtype=jnp.int32)) % 4
    part = attend(ids, cnt, info, kv, kv_far, qs)
    part = lax.all_to_all(
        part.reshape(64, 80, 128), ("x", "head"), split_axis=0, concat_axis=0, tiled=True
    )
    feat, top, bot = mix(part, flat, out_w, gain[None, :], proj_w)
    above = lax.ppermute(bot, "head", [(i, i + 1) for i in range(15)])
    below = lax.ppermute(top, "head", [(i + 1, i) for i in range(15)])
    return dense_head(
        strip[None], feat, above, below, up_w, conv_w.reshape(2, 3, 3 * CH, CH), conv_b
    )


def solution(mesh):
    grid = Mesh(mesh.devices.reshape(2, 4, 16), ("z", "x", "head"))
    rows = ("z", "x")
    in_specs = (
        P(rows, "head", None),
        P(),
        P(),
        P(),
        P(),
        P(),
        P(),
        P(),
        P(rows, None),
        P(rows),
    )
    return jax.shard_map(
        on_device,
        mesh=grid,
        in_specs=in_specs,
        out_specs=P(rows, "head", None, None),
        check_vma=False,
    )
```

time: 417 us -> 191 us (0.46)
  the two profiles are of different devices: /device:TPU:1 before, /device:TPU:97 now
where the time goes in v1:
time: 191 us; the launch traced here: 194 us
  Pallas kernels  96.5 us (51%)
  waiting for transfers between devices  43.2 us (23%)
  blocking collectives  26.3 us (14%)
  starting transfers between devices  23.3 us (12%)
  local copies, waits for them, and re-layouts  2.71 us (1%)
    pallas_call x1, Pallas kernels, attend(): pl.pallas_call(attend_body, in_specs=[smem, smem, smem] + [vmem] * 6, out...  65.1 us
    all_to_all x1, blocking collectives, on_device(): lax.all_to_all(part.reshape(64, 80, 128), ('x', 'head'), split_axis=0, co...  26.3 us
    ppermute x3, waiting for transfers between devices, on_device(): lax.ppermute(q, 'x', [(i, (i + k) % 4) for i in range(4)])  23.5 us
    pallas_call x1, Pallas kernels, dense_head(): pl.pallas_call(head_body, grid=(2,), in_specs=[pl.BlockSpec(memory_space=...  14.4 us
    all_to_all x1, waiting for transfers between devices, on_device(): lax.all_to_all(packed, 'head', split_axis=0, concat_axis=0, tiled=True)  11 us
    pallas_call x1, Pallas kernels, qkv(): pl.pallas_call(qkv_body, grid=(HEADS // 2,), in_specs=[pl.BlockSpec((128,...  10.5 us
    all_to_all x1, starting transfers between devices, on_device(): lax.all_to_all(packed, 'head', split_axis=0, concat_axis=0, tiled=True)  7.86 us
    pallas_call x1, Pallas kernels, mix(): pl.pallas_call(mix_body, out_shape=(jax.ShapeDtypeStruct((128, CH), bf16)...  6.48 us
  transfers between devices with their start and end apart: 10, of which 7 were waited for; matrix products, arithmetic and copies ran while one was open for 2% of the time, Pallas kernels for 0%

profile of v1, /device:TPU:97, one launch (start us, length us, event | category | flops | bytes accessed | tf_op | source)
XLA Modules:
  0.0 194.1 jit_solution(9211029875324074387)
XLA Ops:
  0.0 10.5 %qkv.1 = bf16[16,320,128]{2,1,0:T(8,128)(2,1)} custom-call(f32[128,1024]{1,0:T(8,128)} %bitcast.8, f32[1024,3072]{1,0:T(8,128)} %w_ref.2), custom_call_target="tpu_custom_call" | custom-call | tf_op jit(solution)/shard_map/qkv/pallas_call | solution.py:56
  10.5 7.9 %all-to-all-start = ((bf16[16,320,128]{2,1,0:T(8,128)(2,1)}), bf16[16,320,128]{2,1,0:T(8,128)(2,1)S(1)}, u32[]{:S(2)}, u32[]{:S(2)}) async-start(bf16[16,320,128]{2,1,0:T(8,128)(2,1)} %qkv.1), calls=%async_computation | async-start | bytes 2621440 | tf_op jit(solution)/shard_map/all_to_all | solution.py:364
  18.6 2.5 %collective-permute-start.2 = (s32[16,27]{1,0:T(8,128)S(1)}, s32[16,27]{1,0:T(8,128)S(1)}, u32[]{:S(2)}, u32[]{:S(2)}) collective-permute-start(s32[16,27]{1,0:T(8,128)S(1)} %pad_add_fusion.1), channel_id=1, source_target_pairs={{0,48},{16,0},{32,16},{48,32},{1,49},{17,1},{33,17},{49,33},{2,50}... | collective-permute-start | bytes 5192 | tf_op jit(solution)/shard_map/ppermute | solution.py:342
  21.0 0.5 collective-permute-start.1
  21.6 0.6 collective-permute-start
  22.2 0.6 and_select_fusion.info
  22.8 2.6 %collective-permute-done.1 = s32[16,27]{1,0:T(8,128)S(1)} collective-permute-done((s32[16,27]{1,0:T(8,128)S(1)}, s32[16,27]{1,0:T(8,128)S(1)}, u32[]{:S(2)}, u32[]{:S(2)}) %collective-permute-start.1) | collective-permute-done | bytes 1760 | tf_op jit(solution)/shard_map/ppermute | solution.py:342
  25.6 11.0 %all-to-all-done = bf16[16,320,128]{2,1,0:T(8,128)(2,1)S(1)} async-done(((bf16[16,320,128]{2,1,0:T(8,128)(2,1)}), bf16[16,320,128]{2,1,0:T(8,128)(2,1)S(1)}, u32[]{:S(2)}, u32[]{:S(2)}) %all-to-all-start) | async-done | bytes 1310752 | tf_op jit(solution)/shard_map/all_to_all | solution.py:364
  37.1 2.5 %collective-permute-start.6 = (bf16[16,128,128]{2,1,0:T(8,128)(2,1)S(1)}, bf16[16,128,128]{2,1,0:T(8,128)(2,1)S(1)}, u32[]{:S(2)}, u32[]{:S(2)}) collective-permute-start(bf16[16,128,128]{2,1,0:T(8,128)(2,1)S(1)} %slice.19.q0), channel_id=1, source_target_pairs={{0,48},{16,0},{32,16},{48,32},{1,49},{17,1},{33,17},{49,33},{2,50}... | collective-permute-start | bytes 1572872 | tf_op jit(solution)/shard_map/ppermute | solution.py:368
  40.2 0.6 collective-permute-start.4
  40.8 0.8 convert_reduce_fusion
  42.1 0.7 copy.16.ids
  42.8 8.5 %collective-permute-done.6.q3 = bf16[16,128,128]{2,1,0:T(8,128)(2,1)S(1)} collective-permute-done((bf16[16,128,128]{2,1,0:T(8,128)(2,1)S(1)}, bf16[16,128,128]{2,1,0:T(8,128)(2,1)S(1)}, u32[]{:S(2)}, u32[]{:S(2)}) %collective-permute-start.6) | collective-permute-done | bytes 524320 | tf_op jit(solution)/shard_map/ppermute | solution.py:368
  51.3 2.7 %collective-permute-done.5.q2 = bf16[16,128,128]{2,1,0:T(8,128)(2,1)S(1)} collective-permute-done((bf16[16,128,128]{2,1,0:T(8,128)(2,1)S(1)}, bf16[16,128,128]{2,1,0:T(8,128)(2,1)S(1)}, u32[]{:S(2)}, u32[]{:S(2)}) %collective-permute-start.5) | collective-permute-done | bytes 524320 | tf_op jit(solution)/shard_map/ppermute | solution.py:368
  54.0 12.3 %collective-permute-done.4.q1 = bf16[16,128,128]{2,1,0:T(8,128)(2,1)} collective-permute-done((bf16[16,128,128]{2,1,0:T(8,128)(2,1)S(1)}, bf16[16,128,128]{2,1,0:T(8,128)(2,1)}, u32[]{:S(2)}, u32[]{:S(2)}) %collective-permute-start.4) | collective-permute-done | bytes 524320 | tf_op jit(solution)/shard_map/ppermute | solution.py:368
  66.4 0.9 copy-done.2
  67.3 65.1 %attend.1 = bf16[4,16,80,128]{3,2,1,0:T(8,128)(2,1)} custom-call(s32[64,26]{1,0:T(8,128)} %copy.16.ids, s32[64]{0:T(128)} %get-tuple-element.11.cnt, s32[4]{0:T(128)} %and_select_fusion.info, bf16[16,192,128]{2,1,0:T(8,128)(2,1)} %copy-done, bf16[16,192,128]{2,1,0:T(8,128)(2,1)} %copy-done.2, bf16[16,128,128]{2,1,0:T(8,128)(2,1)} %copy-done.1, ...), custom_call_target="tpu_custom_call" | custom-call | tf_op jit(solution)/shard_map/attend/pallas_call | solution.py:169
  132.4 26.3 %all_to_all.10.r_ref = bf16[64,80,128]{2,1,0:T(8,128)(2,1)} all-to-all(bf16[64,80,128]{2,1,0:T(8,128)(2,1)} %bitcast.6), channel_id=1, replica_groups=mesh['z'=2,'x'=4,'head'=16] {'x','head'}, dimensions={0} | all-to-all | bytes 2621440 | tf_op jit(solution)/shard_map/all_to_all | solution.py:371
  158.7 6.5 %mix.1 = (bf16[128,256]{1,0:T(8,128)(2,1)}, bf16[64,256]{1,0:T(8,128)(2,1)}, bf16[64,256]{1,0:T(8,128)(2,1)}) custom-call(bf16[64,80,128]{2,1,0:T(8,128)(2,1)} %all_to_all.10.r_ref, f32[128,1024]{1,0:T(8,128)} %bitcast.9, f32[1024,1024]{1,0:T(8,128)} %w_ref.3, f32[1,1024]{1,0:T(1,128)} %bitcast.10, f32[1024,256]{1,0:T(8,128)} %proj_ref.1), custom_call_target="tpu_custom_call" | custom-call | tf_op jit(solution)/shard_map/mix/pallas_call | solution.py:229
  165.1 6.1 %collective-permute-start.7 = (bf16[64,256]{1,0:T(8,128)(2,1)}, bf16[64,256]{1,0:T(8,128)(2,1)S(1)}, u32[]{:S(2)}, u32[]{:S(2)}) collective-permute-start(bf16[64,256]{1,0:T(8,128)(2,1)} %get-tuple-element.9), channel_id=1, source_target_pairs={{0,1},{1,2},{2,3},{3,4},{4,5},{5,6},{6,7},{7,8},{8,9},{9,10},{10,1... | collective-permute-start | bytes 98312 | tf_op jit(solution)/shard_map/ppermute | solution.py:375
  171.2 1.9 collective-permute-start.8
  173.2 5.9 %collective-permute-done.8.below_ref = bf16[64,256]{1,0:T(8,128)(2,1)S(1)} collective-permute-done((bf16[64,256]{1,0:T(8,128)(2,1)}, bf16[64,256]{1,0:T(8,128)(2,1)S(1)}, u32[]{:S(2)}, u32[]{:S(2)}) %collective-permute-start.8) | collective-permute-done | bytes 32800 | tf_op jit(solution)/shard_map/ppermute | solution.py:376
  179.1 0.6 copy-done.6
  179.7 14.4 %dense_head.1 = bf16[2,8,128,256]{3,2,1,0:T(8,128)(2,1)} custom-call(s32[1]{0:T(128)} %bitcast.pos, bf16[128,256]{1,0:T(8,128)(2,1)} %get-tuple-element.8.feat_ref, bf16[64,256]{1,0:T(8,128)(2,1)} %copy-done.5, bf16[64,256]{1,0:T(8,128)(2,1)} %copy-done.6, bf16[256,4096]{1,0:T(8,128)(2,1)} %up_ref.1, bf16[2,3,768,256]{3,2,1,0:T(8,128)(2,1)} %bitcast.7, ...), custom_call_target="tpu_custom_call" | custom-call | tf_op jit(solution)/shard_map/dense_head/pallas_call | solution.py:315
  (34 shorter events, 2.0 us)
Async XLA Ops:
  10.5 7.9 %copy-start.8 = (s32[16]{0:T(128)S(1)}, s32[16]{0:T(128)}, u32[]{:S(2)}) copy-start(s32[16]{0:T(128)} %param.19) | copy-start | bytes 196
  10.5 8.0 %copy-start.7 = (s32[16,26]{1,0:T(8,128)S(1)}, s32[16,26]{1,0:T(8,128)}, u32[]{:S(2)}) copy-start(s32[16,26]{1,0:T(8,128)} %param.18) | copy-start | bytes 4996
  10.5 26.1 %all-to-all-start = ((bf16[16,320,128]{2,1,0:T(8,128)(2,1)}), bf16[16,320,128]{2,1,0:T(8,128)(2,1)S(1)}, u32[]{:S(2)}, u32[]{:S(2)}) async-start(bf16[16,320,128]{2,1,0:T(8,128)(2,1)} %qkv.1), calls=%async_computation | async-start | bytes 2621440 | tf_op jit(solution)/shard_map/all_to_all | solution.py:364
  18.6 4.2 %collective-permute-start.2 = (s32[16,27]{1,0:T(8,128)S(1)}, s32[16,27]{1,0:T(8,128)S(1)}, u32[]{:S(2)}, u32[]{:S(2)}) collective-permute-start(s32[16,27]{1,0:T(8,128)S(1)} %pad_add_fusion.1), channel_id=1, source_target_pairs={{0,48},{16,0},{32,16},{48,32},{1,49},{17,1},{33,17},{49,33},{2,50}... | collective-permute-start | bytes 5192 | tf_op jit(solution)/shard_map/ppermute | solution.py:342
  21.0 4.3 %collective-permute-start.1 = (s32[16,27]{1,0:T(8,128)S(1)}, s32[16,27]{1,0:T(8,128)S(1)}, u32[]{:S(2)}, u32[]{:S(2)}) collective-permute-start(s32[16,27]{1,0:T(8,128)S(1)} %pad_add_fusion.1), channel_id=1, source_target_pairs={{0,32},{16,48},{32,0},{48,16},{1,33},{17,49},{33,1},{49,17},{2,34}... | collective-permute-start | bytes 5192 | tf_op jit(solution)/shard_map/ppermute | solution.py:342
  21.6 4.0 %collective-permute-start = (s32[16,27]{1,0:T(8,128)S(1)}, s32[16,27]{1,0:T(8,128)S(1)}, u32[]{:S(2)}, u32[]{:S(2)}) collective-permute-start(s32[16,27]{1,0:T(8,128)S(1)} %pad_add_fusion.1), channel_id=1, source_target_pairs={{0,16},{16,32},{32,48},{48,0},{1,17},{17,33},{33,49},{49,1},{2,18}... | collective-permute-start | bytes 5192 | tf_op jit(solution)/shard_map/ppermute | solution.py:342
  36.7 29.7 %copy-start = (bf16[16,192,128]{2,1,0:T(8,128)(2,1)}, bf16[16,192,128]{2,1,0:T(8,128)(2,1)S(1)}, u32[]{:S(2)}) copy-start(bf16[16,192,128]{2,1,0:T(8,128)(2,1)S(1)} %slice.18.kv0) | copy-start | bytes 2359300
  36.7 29.7 %collective-permute-start.3 = (bf16[16,192,128]{2,1,0:T(8,128)(2,1)S(1)}, bf16[16,192,128]{2,1,0:T(8,128)(2,1)S(1)}, u32[]{:S(2)}, u32[]{:S(2)}) collective-permute-start(bf16[16,192,128]{2,1,0:T(8,128)(2,1)S(1)} %slice.18.kv0), channel_id=1, source_target_pairs={{0,64},{64,0},{1,65},{65,1},{2,66},{66,2},{3,67},{67,3},{4,68},{68... | collective-permute-start | bytes 2359304 | tf_op jit(solution)/shard_map/ppermute | solution.py:367
  37.1 29.3 %copy-start.1 = (bf16[16,128,128]{2,1,0:T(8,128)(2,1)}, bf16[16,128,128]{2,1,0:T(8,128)(2,1)S(1)}, u32[]{:S(2)}) copy-start(bf16[16,128,128]{2,1,0:T(8,128)(2,1)S(1)} %slice.19.q0) | copy-start | bytes 1572868
  37.1 14.2 %collective-permute-start.6 = (bf16[16,128,128]{2,1,0:T(8,128)(2,1)S(1)}, bf16[16,128,128]{2,1,0:T(8,128)(2,1)S(1)}, u32[]{:S(2)}, u32[]{:S(2)}) collective-permute-start(bf16[16,128,128]{2,1,0:T(8,128)(2,1)S(1)} %slice.19.q0), channel_id=1, source_target_pairs={{0,48},{16,0},{32,16},{48,32},{1,49},{17,1},{33,17},{49,33},{2,50}... | collective-permute-start | bytes 1572872 | tf_op jit(solution)/shard_map/ppermute | solution.py:368
  39.7 14.4 %collective-permute-start.5 = (bf16[16,128,128]{2,1,0:T(8,128)(2,1)S(1)}, bf16[16,128,128]{2,1,0:T(8,128)(2,1)S(1)}, u32[]{:S(2)}, u32[]{:S(2)}) collective-permute-start(bf16[16,128,128]{2,1,0:T(8,128)(2,1)S(1)} %slice.19.q0), channel_id=1, source_target_pairs={{0,32},{16,48},{32,0},{48,16},{1,33},{17,49},{33,1},{49,17},{2,34}... | collective-permute-start | bytes 1572872 | tf_op jit(solution)/shard_map/ppermute | solution.py:368
  40.2 26.2 %collective-permute-start.4 = (bf16[16,128,128]{2,1,0:T(8,128)(2,1)S(1)}, bf16[16,128,128]{2,1,0:T(8,128)(2,1)}, u32[]{:S(2)}, u32[]{:S(2)}) collective-permute-start(bf16[16,128,128]{2,1,0:T(8,128)(2,1)S(1)} %slice.19.q0), channel_id=1, source_target_pairs={{0,16},{16,32},{32,48},{48,0},{1,17},{17,33},{33,49},{49,1},{2,18}... | collective-permute-start | bytes 1572872 | tf_op jit(solution)/shard_map/ppermute | solution.py:368
  51.3 15.1 %copy-start.3 = (bf16[16,128,128]{2,1,0:T(8,128)(2,1)}, bf16[16,128,128]{2,1,0:T(8,128)(2,1)S(1)}, u32[]{:S(2)}) copy-start(bf16[16,128,128]{2,1,0:T(8,128)(2,1)S(1)} %collective-permute-done.6.q3) | copy-start | bytes 1572868
  54.0 12.4 %copy-start.4 = (bf16[16,128,128]{2,1,0:T(8,128)(2,1)}, bf16[16,128,128]{2,1,0:T(8,128)(2,1)S(1)}, u32[]{:S(2)}) copy-start(bf16[16,128,128]{2,1,0:T(8,128)(2,1)S(1)} %collective-permute-done.5.q2) | copy-start | bytes 1572868
  66.4 0.9 copy-start.2
  165.1 8.0 %collective-permute-start.7 = (bf16[64,256]{1,0:T(8,128)(2,1)}, bf16[64,256]{1,0:T(8,128)(2,1)S(1)}, u32[]{:S(2)}, u32[]{:S(2)}) collective-permute-start(bf16[64,256]{1,0:T(8,128)(2,1)} %get-tuple-element.9), channel_id=1, source_target_pairs={{0,1},{1,2},{2,3},{3,4},{4,5},{5,6},{6,7},{7,8},{8,9},{9,10},{10,1... | collective-permute-start | bytes 98312 | tf_op jit(solution)/shard_map/ppermute | solution.py:375
  171.2 7.8 %collective-permute-start.8 = (bf16[64,256]{1,0:T(8,128)(2,1)}, bf16[64,256]{1,0:T(8,128)(2,1)S(1)}, u32[]{:S(2)}, u32[]{:S(2)}) collective-permute-start(bf16[64,256]{1,0:T(8,128)(2,1)} %get-tuple-element.10), channel_id=1, source_target_pairs={{1,0},{2,1},{3,2},{4,3},{5,4},{6,5},{7,6},{8,7},{9,8},{10,9},{11,1... | collective-permute-start | bytes 98312 | tf_op jit(solution)/shard_map/ppermute | solution.py:376
  173.2 5.9 %copy-start.5 = (bf16[64,256]{1,0:T(8,128)(2,1)}, bf16[64,256]{1,0:T(8,128)(2,1)S(1)}, u32[]{:S(2)}) copy-start(bf16[64,256]{1,0:T(8,128)(2,1)S(1)} %collective-permute-done.7.above_ref) | copy-start | bytes 98308
  179.1 0.6 copy-start.6
